TPU v7x, 128 devices: a whole 4x4x4 slice. The times are simulated.
128 devices in a mesh: gx: 16 (over y, z_lo, core), gy: 8 (over x, z_hi).
Axes of the slice: x: 4, y: 4, z: 4 (z_hi: 2, z_lo: 2; z = z_hi * 2 + z_lo), core: 2. Of those that a mesh axis runs over, the one named last changes fastest.
Arguments:
- fields: bfloat16 [8, 256, 128, 128], P(None, ('gx', 'gy')), may hold values from -6 to 6
- w_lift: bfloat16 [3, 3, 3, 8, 64], replicated, may hold values from -0.4375 to 0.4375
- b_lift: float32 [64], replicated, may hold values from -3 to 3
- down_weight: bfloat16 [4, 4, 4, 64, 64], replicated, may hold values from -0.09375 to 0.09375
- b_down: float32 [64], replicated, may hold values from -3 to 3
- perf_well: int32 [128, 256], P(('gx', 'gy')), may hold values from -1 to 2047, as said below
- perf_cell: int32 [128, 256], P(('gx', 'gy')), may hold values from 0 to 4095, as said below
- perf_weight: float32 [128, 256], P(('gx', 'gy')), may hold values from 0.25 to 2
- well_slot: int32 [2048], replicated, may hold values from 0 to 2047, each once
- well_grad: bfloat16 [2048, 64], P(('gx', 'gy')), may hold values from -24 to 24
- field_grad: bfloat16 [64, 64, 64, 128], P(None, 'gx', 'gy'), may hold values from -6 to 6
Outputs:
- coarse: bfloat16 [64, 64, 64, 128], P(None, 'gx', 'gy')
- well_feat: float32 [2048, 64], P(('gx', 'gy'))
- down_grad: float32 [4, 4, 4, 64, 64], replicated
Inputs may be any that keep to these rules, and one draw needn't show every extreme that they name: `perf_well`: entry -1 marks an empty slot. Every well appears in exactly 8 slots of one row, the perforations of one vertical well at consecutive depths. Some row has all 256 slots used in every draw. `perf_cell`: local index (x * 8 + y) * 128 + z of the perforated cell in the row's tile of 4 x 8 x 128 coarse cells; 0 in empty slots. `well_slot`: A permutation; row r is held by the device of index r // 16 along gx+gy.
All inputs are finite; a program needn't handle non-finite values.
Results may differ from a plain program's by a relative error of at most 0.0045.
Values may be sent and summed in bfloat16 or wider, within the bound.
No kernel may reach another device: no remote copies, remote signals or barrier semaphores. Data moves between devices by JAX's collectives and lax.ppermute only.
A program may use at most 128 MiB of HBM per device.

v0:
```python
import math
import jax
import jax.numpy as jnp
from jax import lax
from jax.sharding import PartitionSpec as P


def with_halo(array, sides, width):
    for axis, dim in sides:
        devices, length = (lax.axis_size(axis), array.shape[dim])
        up = [(i, (i + 1) % devices) for i in range(devices - 1)]
        down = [(j, i) for i, j in up]
        last = lax.slice_in_dim(array, length - width, length, axis=dim)
        initial = lax.slice_in_dim(array, 0, width, axis=dim)
        before = lax.ppermute(last, axis, up)
        after = lax.ppermute(initial, axis, down)
        array = jnp.concatenate([before, array, after], axis=dim)
    return array


def tile_windows(source, along_dim, pieces, tile_len, margin):
    extent = source.shape
    split_dims = extent[:along_dim] + (pieces, tile_len) + extent[along_dim + 1 :]
    leading_part = lax.slice_in_dim(source, 0, pieces * tile_len, axis=along_dim).reshape(
        split_dims
    )
    trailing = lax.slice_in_dim(source, tile_len, pieces * tile_len + 2 * margin, axis=along_dim)
    padding = [(0, 0)] * source.ndim
    padding[along_dim] = (0, tile_len - 2 * margin)
    trailing = jnp.pad(trailing, padding).reshape(split_dims)
    trailing = lax.slice_in_dim(trailing, 0, 2 * margin, axis=along_dim + 1)
    return jnp.concatenate([leading_part, trailing], axis=along_dim + 1)


def lifting(extended, w_lift, b_lift, out_width, out_height):
    full_depth = extended.shape[3]
    padded = jnp.pad(extended, ((0, 0), (0, 0), (0, 0), (1, 1)))
    channels = w_lift.shape[3]
    outputs = w_lift.shape[4]
    depth_block = min(128, full_depth)
    results = []
    for block_start in range(0, full_depth, depth_block):
        running = jnp.zeros((outputs, out_width, out_height, depth_block), jnp.float32)
        for k in range(3):
            stacked = jnp.concatenate(
                [
                    padded[
                        :,
                        i : i + out_width,
                        j : j + out_height,
                        block_start + k : block_start + k + depth_block,
                    ]
                    for i in range(3)
                    for j in range(3)
                ],
                axis=0,
            )
            kernel_taps = w_lift[:, :, k].reshape(9 * channels, outputs)
            running = running + jnp.einsum(
                "ko,kxyz->oxyz", kernel_taps, stacked, preferred_element_type=jnp.float32
            )
        active = jax.nn.gelu(running + b_lift[:, None, None, None])
        results.append(active.astype(jnp.bfloat16))
    return jnp.concatenate(results, axis=3)


def body(
    fields,
    w_lift,
    b_lift,
    down_weight,
    b_down,
    perf_well,
    perf_cell,
    perf_weight,
    well_slot,
    well_grad,
    field_grad,
):
    grid_gx = lax.axis_size("gx")
    grid_gy = lax.axis_size("gy")
    in_channels, slab_depth, grid_width, grid_height = fields.shape
    tile_width = grid_width // grid_gx
    tile_height = grid_height // grid_gy
    full_depth = slab_depth * grid_gx * grid_gy
    features = w_lift.shape[4]
    margin = 1
    padded = jnp.pad(fields, ((0, 0), (0, 0), (margin, margin), (margin, margin)))
    blocks = tile_windows(
        tile_windows(padded, 2, grid_gx, tile_width, margin), 4, grid_gy, tile_height, margin
    )
    blocks = jnp.transpose(blocks, (2, 4, 0, 1, 3, 5))
    arrived = lax.all_to_all(
        blocks.reshape((grid_gx * grid_gy,) + blocks.shape[2:]),
        ("gx", "gy"),
        split_axis=0,
        concat_axis=0,
        tiled=True,
    )
    arrived = arrived.reshape(blocks.shape)
    columns = jnp.transpose(arrived, (2, 4, 5, 0, 1, 3)).reshape(
        in_channels, tile_width + 2 * margin, tile_height + 2 * margin, full_depth
    )
    hidden = lifting(columns, w_lift, b_lift, tile_width, tile_height)
    rimmed = with_halo(hidden, (("gx", 1), ("gy", 2)), 1)
    half_width = tile_width // 2
    half_height = tile_height // 2
    half_depth = full_depth // 2
    cell_count = half_width * half_height * half_depth
    well_count = well_slot.shape[0]
    listed = perf_well[0]
    cell_ids = perf_cell[0]
    weights = perf_weight[0]
    matches = listed[:, None] == jnp.arange(well_count, dtype=jnp.int32)[None, :]
    out_slots = jnp.sum(jnp.where(matches, well_slot[None, :], 0), axis=1)
    out_slots = jnp.where(listed >= 0, out_slots, -1)
    share_fraction = lax.all_gather(well_grad, ("gx", "gy"), axis=0, tiled=True)
    chosen = out_slots[:, None] == jnp.arange(share_fraction.shape[0], dtype=jnp.int32)[None, :]
    pulled = jnp.dot(
        chosen.astype(jnp.bfloat16), share_fraction, preferred_element_type=jnp.float32
    )
    spread = pulled * weights[:, None]
    flat_grad = field_grad.astype(jnp.float32).reshape(features, cell_count)
    flat_grad = flat_grad.at[:, cell_ids].add(spread.T)
    cotangent = flat_grad.astype(jnp.bfloat16).reshape(
        features, half_width, half_height, half_depth
    )
    stretched = jnp.pad(rimmed, ((0, 0), (0, 0), (0, 0), (1, 1)))
    parity = stretched.reshape(features, half_width + 1, 2, half_height + 1, 2, half_depth + 1, 2)
    parity = jnp.transpose(parity, (2, 4, 6, 0, 1, 3, 5)).reshape(
        8 * features, half_width + 1, half_height + 1, half_depth + 1
    )
    split_weight = down_weight.reshape(2, 2, 2, 2, 2, 2, features, features)
    coarse_sum = jnp.zeros((features, half_width, half_height, half_depth), jnp.float32)
    grad_rows = []
    for a in range(2):
        grad_cols = []
        for b in range(2):
            stacked = jnp.concatenate(
                [
                    parity[:, a : a + half_width, b : b + half_height, depth : depth + half_depth]
                    for depth in range(2)
                ],
                axis=0,
            )
            kernel_taps = jnp.transpose(split_weight[a, :, b], (2, 0, 1, 3, 4, 5)).reshape(
                16 * features, features
            )
            coarse_sum = coarse_sum + jnp.einsum(
                "ko,kxyz->oxyz", kernel_taps, stacked, preferred_element_type=jnp.float32
            )
            grad_part = jnp.einsum(
                "oxyz,kxyz->ko", cotangent, stacked, preferred_element_type=jnp.float32
            )
            grad_cols.append(grad_part.reshape(2, 2, 2, 2, features, features))
        grad_rows.append(jnp.stack(grad_cols))
    local_grad = jnp.transpose(jnp.stack(grad_rows), (0, 3, 1, 4, 2, 5, 6, 7)).reshape(
        4, 4, 4, features, features
    )
    coarse = (coarse_sum + b_down[:, None, None, None]).astype(jnp.bfloat16)
    grad_scale = 1.0 / math.sqrt(cell_count * grid_gx * grid_gy)
    down_grad = lax.psum(local_grad, ("gx", "gy")) * grad_scale
    picked = (
        coarse.reshape(features, cell_count)[:, cell_ids].astype(jnp.float32) * weights[None, :]
    )
    chosen = (
        out_slots[None, :]
        == jnp.arange(well_grad.shape[0] * lax.axis_size(("gx", "gy")), dtype=jnp.int32)[:, None]
    )
    well_feat = lax.psum_scatter(
        jnp.dot(chosen.astype(jnp.float32), picked.T, precision=lax.Precision.HIGHEST),
        ("gx", "gy"),
        scatter_dimension=0,
        tiled=True,
    )
    return (coarse, well_feat, down_grad)


def solution(mesh):
    placed = (
        P(None, ("gx", "gy"), None, None),
        P(),
        P(),
        P(),
        P(),
        P(("gx", "gy"), None),
        P(("gx", "gy"), None),
        P(("gx", "gy"), None),
        P(),
        P(("gx", "gy"), None),
        P(None, "gx", "gy", None),
    )
    return jax.shard_map(
        body,
        mesh=mesh,
        in_specs=placed,
        out_specs=(P(None, "gx", "gy", None), P(("gx", "gy"), None), P()),
        check_vma=False,
    )
```

profile of v0, /device:TPU:0, one launch (start us, length us, event | category | flops | bytes accessed | tf_op | source)
XLA Modules:
  0.0 1417.5 jit_solution(12922795237270653496)
XLA Ops:
  11.7 5.0 reshape.132
  16.7 5.0 reshape.131
  21.7 6.9 maximum_bitcast_fusion
  28.6 5.7 copy.394
  34.3 9.4 reshape.192
  43.8 11.2 all-to-all-start
  56.5 14.0 all-to-all-done
  70.5 8.9 reshape.193
  79.4 5.3 copy.238
  97.5 2.7 fusion.7
  103.1 3.3 collective-permute-start
  106.4 334.4 %all_gather.3 = bf16[2048,64]{1,0:T(8,128)(2,1)} all-gather(bf16[16,64]{1,0:T(8,128)(2,1)S(1)} %copy-done.22), channel_id=1, replica_groups=mesh['gx'=16,'gy'=8] {'gx','gy'}, dimensions={0}, use_global_device_ids=true | all-gather | bytes 264192 | tf_op jit(solution)/shard_map/all_gather | solution.py:117
  448.3 3.1 copy.290
  453.2 5.2 scatter_fusion
  458.3 2.9 convert_element_type.29
  462.6 6.1 collective-permute-start.2
  468.7 3.1 collective-permute-done.3
  474.1 4.5 pad_maximum_fusion.4
  478.5 11.8 copy.382
  490.3 11.5 pad.24.clone
  501.9 24.0 %reshape.136 = bf16[64,5,2,9,2,129,2]{0,6,5,4,3,2,1:T(2,128)(2,1)} reshape(bf16[64,10,18,258]{0,3,2,1:T(8,128)(2,1)} %pad.24.clone) | data formatting | bytes 11888640 | tf_op jit(solution)/shard_map/reshape | solution.py:129
  525.9 30.6 %copy.282 = bf16[2,2,2,64,5,9,129]{6,3,2,1,0,5,4:T(8,128)(2,1)} copy(bf16[2,2,2,64,5,9,129]{3,2,6,1,5,0,4:T(2,128)(2,1)} %bitcast.188) | data formatting | bytes 11888640 | tf_op jit(solution)/shard_map/transpose | solution.py:130
  556.5 27.7 %fusion.51 = (bf16[512,4,8,128]{3,0,2,1:T(8,128)(2,1)S(1)}, bf16[512,4,8,128]{3,0,2,1:T(8,128)(2,1)S(1)}, bf16[512,4,8,128]{3,0,2,1:T(8,128)(2,1)S(1)}, bf16[512...) fusion(bf16[512,5,9,129]{3,0,2,1:T(8,128)(2,1)} %bitcast.187), kind=kLoop, calls=%fused_computation.145 | loop fusion | bytes 67108864 | tf_op jit(solution)/shard_map/slice | solution.py:141
  584.2 6.7 pad_maximum_fusion.2
  591.0 2.3 fusion.61
  593.4 2.3 fusion.60
  600.3 4.0 pad_maximum_fusion
  604.3 5.7 fusion.59
  614.5 4.7 convolution_add_fusion.2
  630.4 132.6 %all-reduce.7.cloned.1.call-done = f32[4,4,4,64,64]{4,3,2,1,0:T(8,128)} async-done(((f32[4,4,4,64,64]{4,3,2,1,0:T(8,128)}), f32[4,4,4,64,64]{4,3,2,1,0:T(8,128)}) %all-reduce.7.cloned.1.call-update) | async-done | bytes 1048592 | tf_op jit(solution)/shard_map/psum | solution.py:162
  762.9 3.3 broadcast_multiply_fusion
  766.2 644.2 %reduce-scatter.2.cloned.1.call-done = f32[16,64]{1,0:T(8,128)} async-done(((f32[2048,64]{1,0:T(8,128)}), f32[16,64]{1,0:T(8,128)}) %reduce-scatter.2.cloned.1.call-update) | async-done | bytes 4112 | tf_op jit(solution)/shard_map/reduce_scatter | solution.py:170
  (136 shorter events, 54.5 us)
Async XLA Ops:
  34.3 20.7 %copy-start.20 = (s32[1,256]{1,0:T(1,128)S(1)}, s32[1,256]{1,0:T(1,128)}, u32[]{:S(2)}) copy-start(s32[1,256]{1,0:T(1,128)} %param.16) | copy-start | bytes 3076
  34.3 20.7 %copy-start.21 = (s32[2048]{0:T(1024)S(1)}, s32[2048]{0:T(1024)}, u32[]{:S(2)}) copy-start(s32[2048]{0:T(1024)} %param.19) | copy-start | bytes 24580
  34.3 21.1 %copy-start.19 = (bf16[3,3,3,8,64]{4,3,2,1,0:T(8,128)(2,1)S(1)}, bf16[3,3,3,8,64]{4,3,2,1,0:T(8,128)(2,1)}, u32[]{:S(2)}) copy-start(bf16[3,3,3,8,64]{4,3,2,1,0:T(8,128)(2,1)} %param.12) | copy-start | bytes 82948
  34.3 21.1 %copy-start.15 = (bf16[4,4,4,64,64]{4,3,2,1,0:T(8,128)(2,1)S(1)}, bf16[4,4,4,64,64]{4,3,2,1,0:T(8,128)(2,1)}, u32[]{:S(2)}) copy-start(bf16[4,4,4,64,64]{4,3,2,1,0:T(8,128)(2,1)} %param.14) | copy-start | bytes 1572868
  43.8 26.7 %all-to-all-start = ((bf16[128,2,1440]{2,1,0:T(2,128)(2,1)}), bf16[128,2,1440]{2,1,0:T(2,128)(2,1)S(1)}, u32[]{:S(2)}, u32[]{:S(2)}) async-start(bf16[128,2,1440]{2,1,0:T(2,128)(2,1)} %reshape.192), calls=%async_computation | async-start | bytes 1572864 | tf_op jit(solution)/shard_map/all_to_all | solution.py:93
  54.9 708.0 %all-reduce.7.cloned.1.call-start = ((), (), s32[]{:S(2)}) async-start(), calls=%async_computation.3 | async-start | bytes 4194304 | tf_op jit(solution)/shard_map/psum | solution.py:162
  100.2 1.7 copy-start
  100.2 6.2 copy-start.22
  101.9 359.3 %collective-permute-start.1 = (bf16[64,1,16,256]{3,0,2,1:T(8,128)(2,1)}, bf16[64,1,16,256]{3,0,2,1:T(8,128)(2,1)S(1)}, u32[]{:S(2)}, u32[]{:S(2)}) collective-permute-start(bf16[64,1,16,256]{3,0,2,1:T(8,128)(2,1)} %get-tuple-element.29), channel_id=1, source_target_pairs={{8,0},{16,8},{24,16},{32,24},{40,32},{48,40},{56,48},{64,56},{72,6... | collective-permute-start | bytes 1572872 | tf_op jit(solution)/shard_map/ppermute | solution.py:16
  103.1 358.1 %collective-permute-start = (bf16[64,1,16,256]{3,0,2,1:T(8,128)(2,1)}, bf16[64,1,16,256]{3,0,2,1:T(8,128)(2,1)S(1)}, u32[]{:S(2)}, u32[]{:S(2)}) collective-permute-start(bf16[64,1,16,256]{3,0,2,1:T(8,128)(2,1)} %get-tuple-element.28), channel_id=1, source_target_pairs={{0,8},{8,16},{16,24},{24,32},{32,40},{40,48},{48,56},{56,64},{64,7... | collective-permute-start | bytes 1572872 | tf_op jit(solution)/shard_map/ppermute | solution.py:15
  446.3 6.9 copy-start.23
  458.3 2.9 copy-start.1
  461.3 10.5 collective-permute-start.3
  462.6 11.5 collective-permute-start.2
  584.2 6.7 copy-start.2
  584.2 6.7 copy-start.4
  584.2 6.7 copy-start.6
  584.2 6.7 copy-start.13
  593.3 2.4 copy-start.11
  593.4 3.5 copy-start.12
  593.4 3.5 copy-start.18
  596.8 2.2 copy-start.9
  596.8 3.5 copy-start.10
  600.3 4.0 copy-start.14
  614.4 796.1 %reduce-scatter.2.cloned.1.call-start = ((), (), s32[]{:S(2)}) async-start(), calls=%async_computation.2 | async-start | bytes 1056768 | tf_op jit(solution)/shard_map/reduce_scatter | solution.py:170
  614.4 4.7 copy-start.7
  614.5 6.1 copy-start.8
  620.5 2.2 copy-start.3
  620.5 3.5 copy-start.5
  620.5 3.5 copy-start.16
  620.5 3.5 copy-start.26
  624.0 3.2 copy-start.24
  (2 other events, 2.3 us)
Sparse Core Ops, SparseCore 0:
  614.5 148.3 all-reduce.6
  765.9 644.5 reduce-scatter.1
where the time goes:
time: 1430 us; the launch traced here: 1420 us
  waiting for transfers between devices  796 us (56%)
  blocking collectives  334 us (23%)
  local copies, waits for them, and re-layouts  178 us (12%)
  other arithmetic  35.6 us (2%)
  matrix products  34.7 us (2%)
  starting transfers between devices  23.2 us (2%)
  between operations  15 us (1%)
    reduce_scatter x1, waiting for transfers between devices, body(): lax.psum_scatter(jnp.dot(chosen.astype(jnp.float32), picked.T, precision=...  644 us
    all_gather x1, blocking collectives, body(): share_fraction = lax.all_gather(well_grad, ('gx', 'gy'), axis=0, tiled=True)  334 us
    psum x1, waiting for transfers between devices, body(): down_grad = lax.psum(local_grad, ('gx', 'gy')) * grad_scale  133 us
    unnamed x83, local copies, waits for them, and re-layouts  48 us
    transpose x1, local copies, waits for them, and re-layouts, body(): jnp.transpose(parity, (2, 4, 6, 0, 1, 3, 5))  30.6 us
  transfers between devices with their start and end apart: 7, of which 5 were waited for; matrix products, arithmetic and copies ran while one was open for 3% of the time, Pallas kernels for 0%

commit v1 on v0

--- a/solution.py
+++ b/solution.py
@@ -114,7 +114,8 @@
     matches = listed[:, None] == jnp.arange(well_count, dtype=jnp.int32)[None, :]
     out_slots = jnp.sum(jnp.where(matches, well_slot[None, :], 0), axis=1)
     out_slots = jnp.where(listed >= 0, out_slots, -1)
-    share_fraction = lax.all_gather(well_grad, ("gx", "gy"), axis=0, tiled=True)
+    outgoing = jnp.stack([well_grad] * lax.axis_size(("gx", "gy")))
+    share_fraction = jnp.concatenate(lax.all_to_all(outgoing, ("gx", "gy"), 0, 0), axis=0)
     chosen = out_slots[:, None] == jnp.arange(share_fraction.shape[0], dtype=jnp.int32)[None, :]
     pulled = jnp.dot(
         chosen.astype(jnp.bfloat16), share_fraction, preferred_element_type=jnp.float32

time: 1430 us -> 1110 us (0.78)
  blocking collectives: 334 us -> 0 us
    all_gather x1 -> x0, blocking collectives: 334 us -> none  [body(): share_fraction = lax.all_gather(well_grad, ('gx', 'gy'), axis=0, tiled=True)]
    unnamed x83 -> x85, local copies, waits for them, and re-layouts: 48 us -> 53 us
  transfers between devices with their start and end apart: 7 -> 8, of which waited for: 5 -> 4; matrix products, arithmetic and copies ran while one was open for 3% -> 7% of each run, Pallas kernels for 0% -> 0%
where the time goes in v1:
time: 1110 us; the launch traced here: 1100 us
  waiting for transfers between devices  798 us (72%)
  local copies, waits for them, and re-layouts  187 us (17%)
  other arithmetic  38.5 us (3%)
  matrix products  34.7 us (3%)
  starting transfers between devices  28.6 us (3%)
  between operations  15 us (1%)
    reduce_scatter x1, waiting for transfers between devices, body(): lax.psum_scatter(jnp.dot(chosen.astype(jnp.float32), picked.T, precision=...  644 us
    psum x1, waiting for transfers between devices, body(): down_grad = lax.psum(local_grad, ('gx', 'gy')) * grad_scale  138 us
    unnamed x85, local copies, waits for them, and re-layouts  53 us
    transpose x1, local copies, waits for them, and re-layouts, body(): jnp.transpose(parity, (2, 4, 6, 0, 1, 3, 5))  30.6 us
    slice x1, local copies, waits for them, and re-layouts, body(): parity[:, a:a + half_width, b:b + half_height, depth:depth + half_depth]  27.6 us
    reshape x1, local copies, waits for them, and re-layouts, body(): stretched.reshape(features, half_width + 1, 2, half_height + 1, 2, half_d...  24 us
  transfers between devices with their start and end apart: 8, of which 4 were waited for; matrix products, arithmetic and copies ran while one was open for 7% of the time, Pallas kernels for 0%

profile of v1, /device:TPU:0, one launch (start us, length us, event | category | flops | bytes accessed | tf_op | source)
XLA Modules:
  0.0 1102.3 jit_solution(10308013215159912877)
XLA Ops:
  11.7 5.0 reshape.137
  16.7 5.0 reshape.136
  21.7 6.9 maximum_bitcast_fusion
  28.6 5.7 copy.394
  34.3 9.3 reshape.198
  43.7 11.2 %all-to-all-start = ((bf16[128,2,1440]{2,1,0:T(2,128)(2,1)}), bf16[128,2,1440]{2,1,0:T(2,128)(2,1)S(1)}, u32[]{:S(2)}, u32[]{:S(2)}) async-start(bf16[128,2,1440]{2,1,0:T(2,128)(2,1)} %reshape.198), calls=%async_computation | async-start | bytes 1572864 | tf_op jit(solution)/shard_map/all_to_all | solution.py:93
  56.4 14.0 %all-to-all-done = bf16[128,2,1440]{2,1,0:T(2,128)(2,1)S(1)} async-done(((bf16[128,2,1440]{2,1,0:T(2,128)(2,1)}), bf16[128,2,1440]{2,1,0:T(2,128)(2,1)S(1)}, u32[]{:S(2)}, u32[]{:S(2)}) %all-to-all-start) | async-done | bytes 737312 | tf_op jit(solution)/shard_map/all_to_all | solution.py:93
  70.4 4.9 all-to-all-start.1
  75.4 8.9 reshape.199
  84.3 5.3 copy.238
  102.4 2.7 fusion.7
  108.1 3.1 collective-permute-start
  126.3 3.1 copy.290
  132.5 6.8 collective-permute-start.2
  142.2 5.1 scatter_fusion
  147.4 2.9 convert_element_type.29
  152.3 5.7 pad_maximum_fusion.4
  158.0 11.8 %copy.382 = bf16[64,10,18,256]{0,3,2,1:T(8,128)(2,1)} copy(bf16[64,10,18,256]{3,0,2,1:T(8,128)(2,1)} %pad_maximum_fusion.4) | data formatting | bytes 11796480
  169.8 11.5 %pad.24.clone = bf16[64,10,18,258]{0,3,2,1:T(8,128)(2,1)} pad(bf16[64,10,18,256]{0,3,2,1:T(8,128)(2,1)} %copy.382, bf16[]{:T(256)} %constant.1.clone.1), padding=0_0x0_0x0_0x1_1 | pad | bytes 11842562 | tf_op jit(solution)/shard_map/jit(_pad)/pad | solution.py:129
  181.4 24.0 %reshape.141 = bf16[64,5,2,9,2,129,2]{0,6,5,4,3,2,1:T(2,128)(2,1)} reshape(bf16[64,10,18,258]{0,3,2,1:T(8,128)(2,1)} %pad.24.clone) | data formatting | bytes 11888640 | tf_op jit(solution)/shard_map/reshape | solution.py:130
  205.4 30.6 %copy.282 = bf16[2,2,2,64,5,9,129]{6,3,2,1,0,5,4:T(8,128)(2,1)} copy(bf16[2,2,2,64,5,9,129]{3,2,6,1,5,0,4:T(2,128)(2,1)} %bitcast.189) | data formatting | bytes 11888640 | tf_op jit(solution)/shard_map/transpose | solution.py:131
  236.0 27.6 %fusion.51 = (bf16[512,4,8,128]{3,0,2,1:T(8,128)(2,1)S(1)}, bf16[512,4,8,128]{3,0,2,1:T(8,128)(2,1)S(1)}, bf16[512,4,8,128]{3,0,2,1:T(8,128)(2,1)S(1)}, bf16[512...) fusion(bf16[512,5,9,129]{3,0,2,1:T(8,128)(2,1)} %bitcast.188), kind=kLoop, calls=%fused_computation.145 | loop fusion | bytes 67108864 | tf_op jit(solution)/shard_map/slice | solution.py:142
  263.6 6.7 pad_maximum_fusion.2
  270.4 2.3 fusion.61
  272.8 2.3 fusion.60
  279.7 4.0 pad_maximum_fusion
  283.7 5.7 fusion.59
  289.5 2.3 fusion.58
  293.9 4.7 convolution_add_fusion.2
  309.7 138.1 %all-reduce.7.cloned.1.call-done = f32[4,4,4,64,64]{4,3,2,1,0:T(8,128)} async-done(((f32[4,4,4,64,64]{4,3,2,1,0:T(8,128)}), f32[4,4,4,64,64]{4,3,2,1,0:T(8,128)}) %all-reduce.7.cloned.1.call-update) | async-done | bytes 1048592 | tf_op jit(solution)/shard_map/psum | solution.py:163
  447.8 3.3 broadcast_multiply_fusion
  451.1 644.2 %reduce-scatter.2.cloned.1.call-done = f32[16,64]{1,0:T(8,128)} async-done(((f32[2048,64]{1,0:T(8,128)}), f32[16,64]{1,0:T(8,128)}) %reduce-scatter.2.cloned.1.call-update) | async-done | bytes 4112 | tf_op jit(solution)/shard_map/reduce_scatter | solution.py:171
  (140 shorter events, 62.5 us)
Async XLA Ops:
  34.3 20.5 %copy-start.22 = (bf16[16,64]{1,0:T(8,128)(2,1)S(1)}, bf16[16,64]{1,0:T(8,128)(2,1)}, u32[]{:S(2)}) copy-start(bf16[16,64]{1,0:T(8,128)(2,1)} %param.20) | copy-start | bytes 6148
  43.7 12.3 %copy-start.20 = (s32[1,256]{1,0:T(1,128)S(1)}, s32[1,256]{1,0:T(1,128)}, u32[]{:S(2)}) copy-start(s32[1,256]{1,0:T(1,128)} %param.16) | copy-start | bytes 3076
  43.7 12.3 %copy-start.21 = (s32[2048]{0:T(1024)S(1)}, s32[2048]{0:T(1024)}, u32[]{:S(2)}) copy-start(s32[2048]{0:T(1024)} %param.19) | copy-start | bytes 24580
  43.7 12.7 %copy-start.19 = (bf16[3,3,3,8,64]{4,3,2,1,0:T(8,128)(2,1)S(1)}, bf16[3,3,3,8,64]{4,3,2,1,0:T(8,128)(2,1)}, u32[]{:S(2)}) copy-start(bf16[3,3,3,8,64]{4,3,2,1,0:T(8,128)(2,1)} %param.12) | copy-start | bytes 82948
  43.7 26.7 %all-to-all-start = ((bf16[128,2,1440]{2,1,0:T(2,128)(2,1)}), bf16[128,2,1440]{2,1,0:T(2,128)(2,1)S(1)}, u32[]{:S(2)}, u32[]{:S(2)}) async-start(bf16[128,2,1440]{2,1,0:T(2,128)(2,1)} %reshape.198), calls=%async_computation | async-start | bytes 1572864 | tf_op jit(solution)/shard_map/all_to_all | solution.py:93
  70.4 68.9 %all-to-all-start.1 = ((bf16[128,2,512]{2,1,0:T(2,128)(2,1)}), bf16[128,2,512]{2,1,0:T(2,128)(2,1)S(1)}, u32[]{:S(2)}, u32[]{:S(2)}) async-start(bf16[128,2,512]{2,1,0:T(2,128)(2,1)} %reshape.200), calls=%async_computation.2 | async-start | bytes 524288 | tf_op jit(solution)/shard_map/all_to_all | solution.py:118
  75.3 372.5 %all-reduce.7.cloned.1.call-start = ((), (), s32[]{:S(2)}) async-start(), calls=%async_computation.4 | async-start | bytes 4194304 | tf_op jit(solution)/shard_map/psum | solution.py:163
  105.1 6.0 copy-start.15
  105.1 7.0 copy-start.23
  106.8 22.6 %collective-permute-start.1 = (bf16[64,1,16,256]{3,0,2,1:T(8,128)(2,1)}, bf16[64,1,16,256]{3,0,2,1:T(8,128)(2,1)S(1)}, u32[]{:S(2)}, u32[]{:S(2)}) collective-permute-start(bf16[64,1,16,256]{3,0,2,1:T(8,128)(2,1)} %get-tuple-element.29), channel_id=1, source_target_pairs={{8,0},{16,8},{24,16},{32,24},{40,32},{48,40},{56,48},{64,56},{72,6... | collective-permute-start | bytes 1572872 | tf_op jit(solution)/shard_map/ppermute | solution.py:16
  108.1 21.3 %collective-permute-start = (bf16[64,1,16,256]{3,0,2,1:T(8,128)(2,1)}, bf16[64,1,16,256]{3,0,2,1:T(8,128)(2,1)S(1)}, u32[]{:S(2)}, u32[]{:S(2)}) collective-permute-start(bf16[64,1,16,256]{3,0,2,1:T(8,128)(2,1)} %get-tuple-element.28), channel_id=1, source_target_pairs={{0,8},{8,16},{16,24},{24,32},{32,40},{40,48},{48,56},{56,64},{64,7... | collective-permute-start | bytes 1572872 | tf_op jit(solution)/shard_map/ppermute | solution.py:15
  131.3 19.0 %collective-permute-start.3 = (bf16[64,10,1,256]{3,0,2,1:T(8,128)(2,1)}, bf16[64,10,1,256]{3,0,2,1:T(8,128)(2,1)}, u32[]{:S(2)}, u32[]{:S(2)}) collective-permute-start(bf16[64,10,1,256]{3,0,2,1:T(8,128)(2,1)} %get-tuple-element.27), channel_id=1, source_target_pairs={{1,0},{2,1},{3,2},{4,3},{5,4},{6,5},{7,6},{9,8},{10,9},{11,10},{12... | collective-permute-start | bytes 983048 | tf_op jit(solution)/shard_map/ppermute | solution.py:16
  132.5 19.8 %collective-permute-start.2 = (bf16[64,10,1,256]{3,0,2,1:T(8,128)(2,1)}, bf16[64,10,1,256]{3,0,2,1:T(8,128)(2,1)}, u32[]{:S(2)}, u32[]{:S(2)}) collective-permute-start(bf16[64,10,1,256]{3,0,2,1:T(8,128)(2,1)} %get-tuple-element.26), channel_id=1, source_target_pairs={{0,1},{1,2},{2,3},{3,4},{4,5},{5,6},{6,7},{8,9},{9,10},{10,11},{11... | collective-permute-start | bytes 983048 | tf_op jit(solution)/shard_map/ppermute | solution.py:15
  147.4 5.0 copy-start.1
  263.6 6.7 copy-start.2
  263.6 6.7 copy-start.4
  263.6 6.7 copy-start.6
  263.6 6.7 copy-start.13
  272.7 2.4 copy-start.11
  272.7 3.5 copy-start.12
  272.8 3.5 copy-start.18
  276.2 2.2 copy-start.9
  276.2 3.5 copy-start.10
  279.7 4.0 copy-start.14
  293.8 801.5 %reduce-scatter.2.cloned.1.call-start = ((), (), s32[]{:S(2)}) async-start(), calls=%async_computation.3 | async-start | bytes 1056768 | tf_op jit(solution)/shard_map/reduce_scatter | solution.py:171
  293.8 4.7 copy-start.7
  293.9 5.9 copy-start.8
  299.8 2.2 copy-start.3
  299.8 3.5 copy-start.5
  299.8 3.5 copy-start.16
  299.8 3.5 copy-start.26
  303.2 3.2 copy-start.24
  (3 other events, 4.0 us)
Sparse Core Ops, SparseCore 0:
  293.9 153.8 all-reduce.6
  450.7 644.5 reduce-scatter.1
